TPU v7x, 32 devices: a whole 2x2x4 slice. The times are simulated.
32 devices in a mesh: dp: 4 (over z), span: 2 (over core), tensor: 4 (over y, x).
Axes of the slice: x: 2, y: 2, z: 4, core: 2. Of those that a mesh axis runs over, the one named last changes fastest.
Arguments:
- layer_input: bfloat16 [2, 16, 512, 768], P('span', 'dp', 'tensor'), may hold values from -6 to 6
- skip_tokens: bfloat16 [2, 16, 512, 768], P('span', 'dp', 'tensor'), may hold values from -6 to 6
- backbone_cotangent: bfloat16 [2, 16, 512, 768], P('span', 'dp', 'tensor'), may hold values from -6 to 6
- head_cotangent: bfloat16 [2, 16, 512, 768], P('span', 'dp', 'tensor'), may hold values from -6 to 6
- segment_lengths: int32 [2, 16, 4], P('span', 'dp'), may hold values from 1 to 174, 464 in all within a row
- pair_index: int32 [64], replicated, may hold values from 0 to 63, each once
- w_heads: bfloat16 [2, 3, 768, 768], P(None, None, None, 'tensor'), may hold values from -0.21875 to 0.21875
- heads_bias: bfloat16 [2, 2, 768], P(None, None, 'tensor'), may hold values from -1.75 to 1.75
- w_project: bfloat16 [2, 768, 768], P(None, 'tensor'), may hold values from -0.875 to 0.875
- project_bias: bfloat16 [2, 768], replicated, may hold values from -1.75 to 1.75
- norm_gain: bfloat16 [2, 2, 768], replicated, may hold values from 0.5 to 1.5
- norm_shift: bfloat16 [2, 2, 768], replicated, may hold values from -1.75 to 1.75
- w_expand: bfloat16 [2, 768, 3072], P(None, None, 'tensor'), may hold values from -0.21875 to 0.21875
- expand_bias: bfloat16 [2, 3072], P(None, 'tensor'), may hold values from -3 to 3
- w_shrink: bfloat16 [2, 3072, 768], P(None, 'tensor'), may hold values from -0.109375 to 0.109375
- shrink_bias: bfloat16 [2, 768], replicated, may hold values from -1.75 to 1.75
Outputs:
- backbone_out: bfloat16 [2, 16, 512, 768], P('span', 'dp', 'tensor')
- head_out: bfloat16 [2, 16, 512, 768], P('span', 'dp', 'tensor')
- span_loss: float32 [], replicated
- grad_input: bfloat16 [2, 16, 512, 768], P('span', 'dp', 'tensor')
- grad_skip: bfloat16 [2, 16, 512, 768], P('span', 'dp', 'tensor')
- grad_heads: float32 [2, 3, 768, 768], P(None, None, None, 'tensor')
- grad_heads_bias: float32 [2, 2, 768], P(None, None, 'tensor')
- grad_project: float32 [2, 768, 768], P(None, 'tensor')
- grad_project_bias: float32 [2, 768], replicated
- grad_gain: float32 [2, 2, 768], replicated
- grad_shift: float32 [2, 2, 768], replicated
- grad_expand: float32 [2, 768, 3072], P(None, None, 'tensor')
- grad_expand_bias: float32 [2, 3072], P(None, 'tensor')
- grad_shrink: float32 [2, 3072, 768], P(None, 'tensor')
- grad_shrink_bias: float32 [2, 768], replicated
Inputs may be any that keep to these rules, and one draw needn't show every extreme that they name: `segment_lengths`: each row holds 4 spans whose lengths add up to 464, the longest being 174; the rest of the row is padding. `pair_index`: each value occurs exactly once.
All inputs are finite; a program needn't handle non-finite values.
Results may differ from a plain program's by a relative error of at most 0.015.
The roundings to bfloat16 on the way count: a program that leaves them out, or rounds other values in their place, can miss the bound.
Values may be sent and summed in bfloat16 or wider, within the bound.
A program may use at most 192 MiB of HBM per device.

v0:
```python
import math
import jax
import jax.numpy as jnp
from jax import lax
from jax.sharding import PartitionSpec as P

HEAD_DIM = 64
EPSILON = 1e-12
LOSS_WEIGHT = 8.0
HIGHEST = lax.Precision.HIGHEST
MASKED = -1e30


def normalize(values, norm_scale, norm_offset):
    centred = values - jnp.mean(values, axis=-1, keepdims=True)
    spread = jnp.mean(centred * centred, axis=-1, keepdims=True)
    return centred * lax.rsqrt(spread + EPSILON) * norm_scale + norm_offset


def activate(values):
    return jax.nn.gelu(values, approximate=False)


def spread_rows(values):
    return lax.all_gather(values, "tensor", axis=1, tiled=True)


def collect_rows(values):
    return lax.psum_scatter(values, "tensor", scatter_dimension=1, tiled=True)


def split_heads(values):
    return values.reshape(values.shape[0], values.shape[1] // HEAD_DIM, HEAD_DIM)


def scores_of(queries, key_rows, segment):
    scores = (
        jnp.einsum("qhd,khd->hqk", queries, key_rows, preferred_element_type=jnp.float32) * 0.125
    )
    same_span = segment[:, None] == segment[None, :]
    return jnp.where(same_span[None], scores, MASKED)


def attend_forward(pieces):
    queries, key_rows, value_rows, segment = pieces
    queries = split_heads(queries)
    key_rows = split_heads(key_rows)
    value_rows = split_heads(value_rows)
    scores = scores_of(queries, key_rows, segment)
    maximum = jnp.max(scores, axis=-1, keepdims=True)
    raised = jnp.exp(scores - maximum)
    row_total = jnp.sum(raised, axis=-1, keepdims=True)
    attention = (raised / row_total).astype(jnp.bfloat16)
    mixture = jnp.einsum("hqk,khd->qhd", attention, value_rows, preferred_element_type=jnp.float32)
    mixture = mixture.reshape(mixture.shape[0], mixture.shape[1] * HEAD_DIM).astype(jnp.bfloat16)
    return (mixture, (maximum + jnp.log(row_total))[..., 0])


def attend_backward(pieces):
    queries, key_rows, value_rows, segment, upward, log_total = pieces
    local_width = queries.shape[1]
    queries = split_heads(queries)
    key_rows = split_heads(key_rows)
    value_rows = split_heads(value_rows)
    upward = split_heads(upward)
    scores = scores_of(queries, key_rows, segment)
    attention = jnp.exp(scores - log_total[..., None])
    grad_weights = jnp.einsum(
        "qhd,khd->hqk", upward, value_rows, preferred_element_type=jnp.float32
    )
    grad_scores = (
        attention * (grad_weights - jnp.sum(attention * grad_weights, axis=-1, keepdims=True))
    ).astype(jnp.bfloat16)
    grad_query = (
        jnp.einsum("hqk,khd->qhd", grad_scores, key_rows, preferred_element_type=jnp.float32)
        * 0.125
    )
    grad_key = (
        jnp.einsum("hqk,qhd->khd", grad_scores, queries, preferred_element_type=jnp.float32) * 0.125
    )
    grad_value = jnp.einsum(
        "hqk,qhd->khd", attention.astype(jnp.bfloat16), upward, preferred_element_type=jnp.float32
    )
    grad_query = grad_query.reshape(grad_query.shape[0], local_width).astype(jnp.bfloat16)
    grad_key = grad_key.reshape(grad_key.shape[0], local_width).astype(jnp.bfloat16)
    grad_value = grad_value.reshape(grad_value.shape[0], local_width).astype(jnp.bfloat16)
    return (grad_query, grad_key, grad_value)


def layer_forward(share, segment, weights):
    (
        w_heads,
        heads_bias,
        w_project,
        project_bias,
        norm_gain,
        norm_shift,
        w_expand,
        expand_bias,
        w_shrink,
        shrink_bias,
    ) = weights
    rows_in = spread_rows(share.astype(jnp.bfloat16))
    projected = jnp.einsum("std,cde->cste", rows_in, w_heads, preferred_element_type=jnp.float32)
    queries = (projected[0] + heads_bias[0]).astype(jnp.bfloat16)
    key_rows = projected[1].astype(jnp.bfloat16)
    value_rows = (projected[2] + heads_bias[1]).astype(jnp.bfloat16)
    mixture, log_total = lax.map(attend_forward, (queries, key_rows, value_rows, segment))
    first_sum = (
        share
        + collect_rows(
            jnp.einsum("ste,ed->std", mixture, w_project, preferred_element_type=jnp.float32)
        )
        + project_bias
    )
    first_norm = normalize(first_sum, norm_gain[0], norm_shift[0])
    rows_mid = spread_rows(first_norm.astype(jnp.bfloat16))
    expanded = (
        jnp.einsum("std,df->stf", rows_mid, w_expand, preferred_element_type=jnp.float32)
        + expand_bias
    )
    activated = activate(expanded).astype(jnp.bfloat16)
    second_sum = (
        first_norm
        + collect_rows(
            jnp.einsum("stf,fd->std", activated, w_shrink, preferred_element_type=jnp.float32)
        )
        + shrink_bias
    )
    stored = (
        rows_in,
        queries,
        key_rows,
        value_rows,
        mixture,
        log_total,
        first_sum,
        rows_mid,
        expanded,
        activated,
        second_sum,
    )
    return (normalize(second_sum, norm_gain[1], norm_shift[1]), stored)


def layer_backward(upward, segment, weights, stored):
    (
        w_heads,
        heads_bias,
        w_project,
        project_bias,
        norm_gain,
        norm_shift,
        w_expand,
        expand_bias,
        w_shrink,
        shrink_bias,
    ) = weights
    (
        rows_in,
        queries,
        key_rows,
        value_rows,
        mixture,
        log_total,
        first_sum,
        rows_mid,
        expanded,
        activated,
        second_sum,
    ) = stored
    ignored, pull_second = jax.vjp(
        normalize, second_sum, norm_gain[1].astype(jnp.float32), norm_shift[1].astype(jnp.float32)
    )
    grad_second, gain_second, shift_second = pull_second(upward)
    rounded = spread_rows(grad_second.astype(jnp.bfloat16))
    grad_shrink = jnp.einsum("stf,std->fd", activated, rounded, preferred_element_type=jnp.float32)
    grad_act = jnp.einsum("std,fd->stf", rounded, w_shrink, preferred_element_type=jnp.float32)
    ignored, pull_act = jax.vjp(activate, expanded)
    grad_hidden = pull_act(grad_act)[0]
    hidden_low = grad_hidden.astype(jnp.bfloat16)
    grad_expand = jnp.einsum(
        "std,stf->df", rows_mid, hidden_low, preferred_element_type=jnp.float32
    )
    grad_first = grad_second + collect_rows(
        jnp.einsum("stf,df->std", hidden_low, w_expand, preferred_element_type=jnp.float32)
    )
    ignored, pull_first = jax.vjp(
        normalize, first_sum, norm_gain[0].astype(jnp.float32), norm_shift[0].astype(jnp.float32)
    )
    grad_attend, gain_first, shift_first = pull_first(grad_first)
    rounded = spread_rows(grad_attend.astype(jnp.bfloat16))
    grad_project = jnp.einsum("ste,std->ed", mixture, rounded, preferred_element_type=jnp.float32)
    grad_mixture = jnp.einsum(
        "std,ed->ste", rounded, w_project, preferred_element_type=jnp.float32
    ).astype(jnp.bfloat16)
    grad_query, grad_key, grad_value = lax.map(
        attend_backward, (queries, key_rows, value_rows, segment, grad_mixture, log_total)
    )
    grad_heads = jnp.stack(
        [
            jnp.einsum("std,ste->de", rows_in, grad_query, preferred_element_type=jnp.float32),
            jnp.einsum("std,ste->de", rows_in, grad_key, preferred_element_type=jnp.float32),
            jnp.einsum("std,ste->de", rows_in, grad_value, preferred_element_type=jnp.float32),
        ]
    )
    grad_heads_bias = jnp.stack(
        [
            jnp.sum(grad_query.astype(jnp.float32), axis=(0, 1)),
            jnp.sum(grad_value.astype(jnp.float32), axis=(0, 1)),
        ]
    )
    back_terms = jnp.einsum(
        "ste,de->std", grad_query, w_heads[0], preferred_element_type=jnp.float32
    )
    back_terms = back_terms + jnp.einsum(
        "ste,de->std", grad_key, w_heads[1], preferred_element_type=jnp.float32
    )
    back_terms = back_terms + jnp.einsum(
        "ste,de->std", grad_value, w_heads[2], preferred_element_type=jnp.float32
    )
    grad_layer_in = grad_attend + collect_rows(back_terms)
    matrices = (
        grad_heads,
        grad_heads_bias,
        grad_project,
        grad_expand,
        jnp.sum(grad_hidden, axis=(0, 1)),
        grad_shrink,
    )
    vectors = (
        jnp.sum(grad_attend, axis=(0, 1)),
        jnp.stack([gain_first, gain_second]),
        jnp.stack([shift_first, shift_second]),
        jnp.sum(grad_second, axis=(0, 1)),
    )
    return (grad_layer_in, matrices, vectors)


def shards(
    layer_input,
    skip_tokens,
    backbone_cotangent,
    head_cotangent,
    segment_lengths,
    pair_index,
    w_heads,
    heads_bias,
    w_project,
    project_bias,
    norm_gain,
    norm_shift,
    w_expand,
    expand_bias,
    w_shrink,
    shrink_bias,
):
    stacked = (
        w_heads,
        heads_bias,
        w_project,
        project_bias,
        norm_gain,
        norm_shift,
        w_expand,
        expand_bias,
        w_shrink,
        shrink_bias,
    )
    backbone_weights = tuple((member[0] for member in stacked))
    head_weights = tuple((member[1] for member in stacked))
    lengths = segment_lengths[0]
    seq_count = lengths.shape[0]
    span_count = lengths.shape[1]
    share_rows = layer_input.shape[2]
    row_tokens = share_rows * lax.axis_size("tensor")
    starts = jnp.cumsum(lengths, axis=-1) - lengths
    row_length = jnp.sum(lengths, axis=-1)
    places = jnp.arange(row_tokens, dtype=jnp.int32)
    counted = jnp.sum((places[None, :, None] >= starts[:, None, :]).astype(jnp.int32), axis=-1) - 1
    segment = jnp.where(places[None, :] < row_length[:, None], counted, span_count)
    local_places = lax.axis_index("tensor") * share_rows + jnp.arange(share_rows, dtype=jnp.int32)
    valid_rows = (local_places[None, :] < row_length[:, None]).astype(jnp.float32)[..., None]
    picker = (starts[:, :, None] == local_places[None, None, :]).astype(jnp.float32)
    first_mark = jnp.sum(picker, axis=1)[..., None] > 0
    backbone, backbone_stored = layer_forward(
        layer_input[0].astype(jnp.float32), segment, backbone_weights
    )
    chosen = jnp.einsum("sgp,spd->sgd", picker, backbone, precision=HIGHEST)
    slot_count = seq_count * span_count
    feature_count = chosen.shape[2]
    gathered = lax.all_gather(
        chosen.reshape(slot_count, feature_count).astype(jnp.bfloat16),
        ("dp", "span", "tensor"),
        axis=0,
        tiled=True,
    )
    dp_count = lax.axis_size("dp")
    pair_count = lax.axis_size("span")
    tensor_count = lax.axis_size("tensor")
    anchor_rows = jnp.sum(
        gathered.astype(jnp.float32).reshape(
            dp_count, pair_count, tensor_count, slot_count, feature_count
        ),
        axis=2,
    )
    anchor_rows = jnp.transpose(anchor_rows, (1, 0, 2, 3)).reshape(
        pair_count, dp_count * slot_count, feature_count
    )
    head_input = jnp.where(first_mark, backbone, skip_tokens[0].astype(jnp.float32))
    head_rows, head_stored = layer_forward(head_input, segment, head_weights)
    vector_count = dp_count * slot_count
    side_index = lax.axis_index("span")
    block_start = lax.axis_index("dp") * slot_count
    columns = jnp.arange(vector_count, dtype=jnp.int32)
    root_width = math.sqrt(feature_count)
    logits = jnp.dot(anchor_rows[0], anchor_rows[1].T, precision=HIGHEST) / root_width
    target = (pair_index[:, None] == columns[None, :]).astype(jnp.float32)
    lse_rows = jax.nn.logsumexp(logits, axis=1)
    lse_columns = jax.nn.logsumexp(logits, axis=0)
    grad_logits = LOSS_WEIGHT * (
        jnp.exp(logits - lse_rows[:, None]) + jnp.exp(logits - lse_columns[None, :]) - 2.0 * target
    )
    grad_zero = jnp.dot(grad_logits, anchor_rows[1], precision=HIGHEST) / root_width
    grad_one = jnp.dot(grad_logits.T, anchor_rows[0], precision=HIGHEST) / root_width
    both_sides = jnp.stack([grad_zero, grad_one])
    grad_vectors = lax.dynamic_slice(
        lax.dynamic_index_in_dim(both_sides, side_index, 0, keepdims=False),
        (block_start, 0),
        (slot_count, feature_count),
    )
    span_loss = (jnp.sum(lse_rows) + jnp.sum(lse_columns) - 2.0 * jnp.sum(target * logits)) / (
        2 * vector_count
    )
    head_seed = head_cotangent[0].astype(jnp.float32) * valid_rows
    grad_head_in, head_matrices, head_vectors = layer_backward(
        head_seed, segment, head_weights, head_stored
    )
    grad_skip = jnp.where(first_mark, 0.0, grad_head_in)
    from_span = jnp.einsum(
        "sgp,sgd->spd",
        picker,
        grad_vectors.reshape(seq_count, span_count, feature_count),
        precision=HIGHEST,
    )
    backbone_seed = (
        backbone_cotangent[0].astype(jnp.float32) * valid_rows
        + jnp.where(first_mark, grad_head_in, 0.0)
        + from_span
    )
    grad_input, backbone_matrices, backbone_vectors = layer_backward(
        backbone_seed, segment, backbone_weights, backbone_stored
    )
    summed = lax.psum(
        (
            backbone_matrices[0],
            backbone_matrices[1],
            backbone_matrices[2],
            backbone_matrices[3],
            backbone_matrices[4],
            backbone_matrices[5],
            head_matrices[0],
            head_matrices[1],
            head_matrices[2],
            head_matrices[3],
            head_matrices[4],
            head_matrices[5],
        ),
        ("dp", "span"),
    )
    backbone_matrices = summed[:6]
    head_matrices = summed[6:]
    summed_small = lax.psum(
        (
            backbone_vectors[0],
            backbone_vectors[1],
            backbone_vectors[2],
            backbone_vectors[3],
            head_vectors[0],
            head_vectors[1],
            head_vectors[2],
            head_vectors[3],
        ),
        ("dp", "span", "tensor"),
    )
    backbone_vectors = summed_small[:4]
    head_vectors = summed_small[4:]
    return (
        (backbone * valid_rows).astype(jnp.bfloat16)[None],
        (head_rows * valid_rows).astype(jnp.bfloat16)[None],
        span_loss,
        grad_input.astype(jnp.bfloat16)[None],
        grad_skip.astype(jnp.bfloat16)[None],
        jnp.stack([backbone_matrices[0], head_matrices[0]]),
        jnp.stack([backbone_matrices[1], head_matrices[1]]),
        jnp.stack([backbone_matrices[2], head_matrices[2]]),
        jnp.stack([backbone_vectors[0], head_vectors[0]]),
        jnp.stack([backbone_vectors[1], head_vectors[1]]),
        jnp.stack([backbone_vectors[2], head_vectors[2]]),
        jnp.stack([backbone_matrices[3], head_matrices[3]]),
        jnp.stack([backbone_matrices[4], head_matrices[4]]),
        jnp.stack([backbone_matrices[5], head_matrices[5]]),
        jnp.stack([backbone_vectors[3], head_vectors[3]]),
    )


def solution(mesh):
    in_specs = (
        P("span", "dp", "tensor", None),
        P("span", "dp", "tensor", None),
        P("span", "dp", "tensor", None),
        P("span", "dp", "tensor", None),
        P("span", "dp", None),
        P(),
        P(None, None, None, "tensor"),
        P(None, None, "tensor"),
        P(None, "tensor", None),
        P(),
        P(),
        P(),
        P(None, None, "tensor"),
        P(None, "tensor"),
        P(None, "tensor", None),
        P(),
    )
    out_specs = (
        P("span", "dp", "tensor", None),
        P("span", "dp", "tensor", None),
        P(),
        P("span", "dp", "tensor", None),
        P("span", "dp", "tensor", None),
        P(None, None, None, "tensor"),
        P(None, None, "tensor"),
        P(None, "tensor", None),
        P(),
        P(),
        P(),
        P(None, None, "tensor"),
        P(None, "tensor"),
        P(None, "tensor", None),
        P(),
    )
    return jax.shard_map(shards, mesh=mesh, in_specs=in_specs, out_specs=out_specs, check_vma=False)
```

profile of v0, /device:TPU:0, one launch (start us, length us, event | category | flops | bytes accessed | tf_op | source)
XLA Modules:
  0.0 1523.2 jit_solution(11413857618912558488)
XLA Ops:
  11.2 45.2 %all-gather.24.cloned.1.call-done = bf16[1,4,512,768]{3,2,1,0:T(8,128)(2,1)} async-done(((bf16[1,4,128,768]{3,2,1,0:T(8,128)(2,1)}), bf16[1,4,512,768]{3,2,1,0:T(8,128)(2,1)}) %all-gather.24.cloned.1.call-update) | async-done | bytes 3145744 | tf_op jit(solution)/shard_map/all_gather | solution.py:25
  56.4 4.2 fusion.48
  61.1 11.7 while.52
  72.8 4.9 fusion.140
  78.6 69.4 %reduce-scatter.9.cloned.1.call-done = f32[4,128,768]{2,1,0:T(8,128)} async-done(((f32[4,512,768]{2,1,0:T(8,128)}), f32[4,128,768]{2,1,0:T(8,128)}) %reduce-scatter.9.cloned.1.call-update) | async-done | bytes 1572880 | tf_op jit(solution)/shard_map/reduce_scatter | solution.py:29
  151.6 43.7 %all-gather.10.cloned.1.call-done = bf16[4,512,768]{2,1,0:T(8,128)(2,1)} async-done(((bf16[4,128,768]{2,1,0:T(8,128)(2,1)}), bf16[4,512,768]{2,1,0:T(8,128)(2,1)}) %all-gather.10.cloned.1.call-update) | async-done | bytes 3145744 | tf_op jit(solution)/shard_map/all_gather | solution.py:25
  195.3 6.4 fusion.80
  201.8 15.4 %multiply_convert_fusion.3 = (bf16[4,512,768]{2,1,0:T(8,128)(2,1)S(1)}, f32[4,512,768]{2,1,0:T(8,128)}) fusion(f32[4,512,768]{2,1,0:T(8,128)S(1)} %get-tuple-element.398, f32[768]{0:T(1024)S(1)} %get-tuple-element.243, u8[512,768]{1,0:T(8,128)(4,1)S(1)} %get-tuple-element.212, u8[512,768]{1,0:T(8,128)(4,1)S(1)} %get-tuple-element.211), kind=kLoop, calls=%fused_computation.102 | loop fusion | flops 111673344 | bytes 16518144 | tf_op jit(solution)/shard_map/convert_element_type | solution.py:122
  218.8 4.5 fusion.100
  224.1 69.4 %reduce-scatter.11.cloned.1.call-done = f32[4,128,768]{2,1,0:T(8,128)} async-done(((f32[4,512,768]{2,1,0:T(8,128)}), f32[4,128,768]{2,1,0:T(8,128)}) %reduce-scatter.11.cloned.1.call-update) | async-done | bytes 1572880 | tf_op jit(solution)/shard_map/reduce_scatter | solution.py:29
  293.5 2.0 fusion.174
  298.6 43.7 %all-gather.12.cloned.1.call-done = bf16[4,512,768]{2,1,0:T(8,128)(2,1)} async-done(((bf16[4,128,768]{2,1,0:T(8,128)(2,1)}), bf16[4,512,768]{2,1,0:T(8,128)(2,1)}) %all-gather.12.cloned.1.call-update) | async-done | bytes 3145744 | tf_op jit(solution)/shard_map/all_gather | solution.py:25
  342.4 3.9 fusion.51
  347.9 19.1 %while.53 = (s32[]{:T(128)}, bf16[4,512,192]{1,2,0:T(8,128)(2,1)S(1)}, f32[4,3,512]{2,1,0:T(4,128)S(1)}, bf16[4,512,192]{1,2,0:T(8,128)(2,1)}, s32[4,512]{1,0:T(...) while((s32[]{:T(128)}, bf16[4,512,192]{1,2,0:T(8,128)(2,1)S(1)}, ...), condition=%wide.region_17.18_spmd, body=%wide.region_14.17_spmd.sunk | while | flops 211122688 | bytes 12906601 | solution.py:108
  367.0 4.8 fusion.137
  372.0 70.0 %reduce-scatter.13.cloned.1.call-done = f32[4,128,768]{2,1,0:T(8,128)} async-done(((f32[4,512,768]{2,1,0:T(8,128)}), f32[4,128,768]{2,1,0:T(8,128)}) %reduce-scatter.13.cloned.1.call-update) | async-done | bytes 1572880 | tf_op jit(solution)/shard_map/reduce_scatter | solution.py:29
  442.0 3.2 fusion.173
  447.0 43.7 %all-gather.14.cloned.1.call-done = bf16[4,512,768]{2,1,0:T(8,128)(2,1)} async-done(((bf16[4,128,768]{2,1,0:T(8,128)(2,1)}), bf16[4,512,768]{2,1,0:T(8,128)(2,1)}) %all-gather.14.cloned.1.call-update) | async-done | bytes 3145744 | tf_op jit(solution)/shard_map/all_gather | solution.py:25
  490.7 6.4 fusion.81
  497.2 15.4 %multiply_convert_fusion.2 = (bf16[4,512,768]{2,1,0:T(8,128)(2,1)S(1)}, f32[4,512,768]{2,1,0:T(8,128)}) fusion(f32[4,512,768]{2,1,0:T(8,128)S(1)} %get-tuple-element.399, f32[768]{0:T(1024)S(1)} %get-tuple-element.242, u8[512,768]{1,0:T(8,128)(4,1)S(1)} %get-tuple-element.210, u8[512,768]{1,0:T(8,128)(4,1)S(1)} %get-tuple-element.209), kind=kLoop, calls=%fused_computation.89 | loop fusion | flops 111673344 | bytes 16518144 | tf_op jit(solution)/shard_map/convert_element_type | solution.py:122
  514.3 4.5 fusion.94
  518.8 70.1 %reduce-scatter.15.cloned.1.call-done = f32[4,128,768]{2,1,0:T(8,128)} async-done(((f32[4,512,768]{2,1,0:T(8,128)}), f32[4,128,768]{2,1,0:T(8,128)}) %reduce-scatter.15.cloned.1.call-update) | async-done | bytes 1572880 | tf_op jit(solution)/shard_map/reduce_scatter | solution.py:29
  589.0 2.0 fusion.171
  594.5 43.5 %all-gather.16.cloned.1.call-done = bf16[4,512,768]{2,1,0:T(8,128)(2,1)} async-done(((bf16[4,128,768]{2,1,0:T(8,128)(2,1)}), bf16[4,512,768]{2,1,0:T(8,128)(2,1)}) %all-gather.16.cloned.1.call-update) | async-done | bytes 3145744 | tf_op jit(solution)/shard_map/all_gather | solution.py:25
  638.0 11.2 fusion.179
  650.9 4.5 fusion.76
  655.5 70.1 %reduce-scatter.17.cloned.1.call-done = f32[4,128,768]{2,1,0:T(8,128)} async-done(((f32[4,512,768]{2,1,0:T(8,128)}), f32[4,128,768]{2,1,0:T(8,128)}) %reduce-scatter.17.cloned.1.call-update) | async-done | bytes 1572880 | tf_op jit(solution)/shard_map/reduce_scatter | solution.py:29
  725.6 4.6 add_reduce_fusion.3
  734.0 43.8 %all-gather.18.cloned.1.call-done = bf16[4,512,768]{2,1,0:T(8,128)(2,1)} async-done(((bf16[4,128,768]{2,1,0:T(8,128)(2,1)}), bf16[4,512,768]{2,1,0:T(8,128)(2,1)}) %all-gather.18.cloned.1.call-update) | async-done | bytes 3145744 | tf_op jit(solution)/shard_map/all_gather | solution.py:25
  777.7 3.9 convolution_convert_fusion.1
  782.8 36.0 %while.54 = (s32[]{:T(128)}, bf16[4,512,192]{1,2,0:T(8,128)(2,1)S(1)}, bf16[4,512,192]{1,2,0:T(8,128)(2,1)}, bf16[4,512,192]{1,2,0:T(8,128)(2,1)S(1)}, bf16[4,51...) while((s32[]{:T(128)}, ...), condition=%wide.region_39.40_spmd, body=%wide.region_37.39_spmd.sunk | while | flops 511146496 | bytes 28873352 | solution.py:197
  818.8 2.8 fusion.132
  821.6 2.0 fusion.134
  823.6 4.7 add_add_fusion.1
  829.4 74.0 %all_gather.31 = bf16[512,768]{1,0:T(8,128)(2,1)S(1)} all-gather(bf16[16,768]{1,0:T(8,128)(2,1)S(1)} %convert_element_type.392), channel_id=1, replica_groups=mesh['dp'=4,'span'=2,'tensor'=4] {'dp','span','tensor'}, dimensions={0}, use_global_device_ids=true | all-gather | bytes 811008 | tf_op jit(solution)/shard_map/all_gather | solution.py:292
  906.3 4.8 reduce-scatter.19.cloned.1.call-done
  911.1 3.5 multiply_reduce_fusion.3
  916.6 43.7 %all-gather.20.cloned.1.call-done = bf16[4,512,768]{2,1,0:T(8,128)(2,1)} async-done(((bf16[4,128,768]{2,1,0:T(8,128)(2,1)}), bf16[4,512,768]{2,1,0:T(8,128)(2,1)}) %all-gather.20.cloned.1.call-update) | async-done | bytes 3145744 | tf_op jit(solution)/shard_map/all_gather | solution.py:25
  960.3 10.6 fusion.180
  972.6 4.5 fusion.73
  977.3 70.1 %reduce-scatter.21.cloned.1.call-done = f32[4,128,768]{2,1,0:T(8,128)} async-done(((f32[4,512,768]{2,1,0:T(8,128)}), f32[4,128,768]{2,1,0:T(8,128)}) %reduce-scatter.21.cloned.1.call-update) | async-done | bytes 1572880 | tf_op jit(solution)/shard_map/reduce_scatter | solution.py:29
  1047.4 2.2 multiply_reduce_fusion.4
  1053.0 6.1 convolution_bitcast_fusion
  1059.1 4.2 convolution_bitcast_fusion.2
  1071.5 4.2 convolution_bitcast_fusion.1
  1075.7 4.4 convolution_bitcast_fusion.3
  1080.1 16.4 %all-gather.22.cloned.1.call-done = bf16[4,512,768]{2,1,0:T(8,128)(2,1)} async-done(((bf16[4,128,768]{2,1,0:T(8,128)(2,1)}), bf16[4,512,768]{2,1,0:T(8,128)(2,1)}) %all-gather.22.cloned.1.call-update) | async-done | bytes 3145744 | tf_op jit(solution)/shard_map/all_gather | solution.py:25
  1096.5 4.0 convolution_convert_fusion
  1103.3 41.8 %while.55 = (s32[]{:T(128)}, bf16[4,512,192]{1,2,0:T(8,128)(2,1)}, bf16[4,512,192]{1,2,0:T(8,128)(2,1)}, bf16[4,512,192]{1,2,0:T(8,128)(2,1)}, bf16[4,512,192]{1...) while((s32[]{:T(128)}, bf16[4,512,192]{1,2,0:T(8,128)(2,1)}, ...), condition=%wide.region_48.49_spmd, body=%wide.region_46.48_spmd.sunk | while | flops 511146496 | bytes 28873860 | solution.py:197
  1145.1 1.9 fusion.84
  1147.0 2.0 fusion.87
  1154.6 2.0 fusion.127
  1156.6 2.3 fusion.129
  1159.0 4.8 add_add_fusion
  1167.6 2.6 fusion.123
  1170.3 41.6 %all-reduce = (f32[1,768]{1,0:T(1,128)S(1)}, f32[1,768]{1,0:T(1,128)S(1)}, f32[1,2,768]{2,1,0:T(2,128)S(1)}, f32[1,2,768]{2,1,0:T(2,128)S(1)}, f32[1,2,768]{2,1,...) all-reduce(f32[1,768]{1,0:T(1,128)S(1)} %stack.204, ...), channel_id=1, replica_groups=mesh['dp'=4,'span'=2,'tensor'=4] {'dp','span','tensor'}, use_global_device_ids=true, to_apply=%region_63.64 | all-reduce | flops 9216 | bytes 73728 | tf_op jit(solution)/shard_map/psum | solution.py:373
  1215.8 29.2 %all-reduce.1 = (f32[1,2,192]{2,1,0:T(2,128)S(1)}, f32[1,2,192]{2,1,0:T(2,128)S(1)}, f32[1,768]{1,0:T(1,128)S(1)}, f32[1,768]{1,0:T(1,128)S(1)}) all-reduce(f32[1,2,192]{2,1,0:T(2,128)S(1)} %maximum_bitcast_fusion.7, f32[1,2,192]{2,1,0:T(2,128)S(1)} %maximum_bitcast_fusion.6, ...), channel_id=1, replica_groups=mesh['dp'=4,'span'=2,'tensor'=4] {'dp','span'}, use_global_device_ids=true, to_apply=%region_57.58 | all-reduce | flops 2304 | bytes 18432 | tf_op jit(solution)/shard_map/psum | solution.py:354
  1246.2 193.6 %all-reduce.5.cloned.1.call-done = (f32[1,3,768,192]{2,3,1,0:T(8,128)}, f32[1,3,768,192]{2,3,1,0:T(8,128)}, f32[1,192,768]{2,1,0:T(8,128)}, f32[1,192,768]{2,1,0...) async-done(((f32[1,3,768,192]{2,3,1,0:T(8,128)}, f32[1,3,768,192]{2,3,1,0:T(8,128)}, ...) | async-done | bytes 14155792 | tf_op jit(solution)/shard_map/psum | solution.py:354
  1439.8 2.5 pad_maximum_fusion.3
  1442.2 3.7 pad_maximum_fusion.2
  1446.0 2.7 pad_maximum_fusion.1
  1450.5 2.5 pad_maximum_fusion
  1453.0 59.9 %reduce-scatter.23.cloned.1.call-done = f32[4,128,768]{2,1,0:T(8,128)} async-done(((f32[4,512,768]{2,1,0:T(8,128)}), f32[4,128,768]{2,1,0:T(8,128)}) %reduce-scatter.23.cloned.1.call-update) | async-done | bytes 1572880 | tf_op jit(solution)/shard_map/reduce_scatter | solution.py:29
  1512.8 2.5 fusion.122
  (501 shorter events, 172.8 us)
Async XLA Ops:
  7.2 49.3 %all-gather.24.cloned.1.call-start = ((), (), s32[]{:S(2)}) async-start(), calls=%async_computation.23 | async-start | bytes 3932160 | tf_op jit(solution)/shard_map/all_gather | solution.py:25
  7.9 140.1 %reduce-scatter.9.cloned.1.call-start = ((), (), s32[]{:S(2)}) async-start(), calls=%async_computation.8 | async-start | bytes 7864320 | tf_op jit(solution)/shard_map/reduce_scatter | solution.py:29
  72.8 4.9 copy-start.22
  72.8 4.9 copy-start.24
  72.8 4.9 copy-start.26
  72.8 4.9 copy-start.27
  72.8 4.9 copy-start.46
  77.8 70.2 %copy-start.36 = (bf16[1,4,128,768]{3,2,1,0:T(8,128)(2,1)S(1)}, bf16[1,4,128,768]{3,2,1,0:T(8,128)(2,1)}, u32[]{:S(2)}) copy-start(bf16[1,4,128,768]{3,2,1,0:T(8,128)(2,1)} %param.24) | copy-start | bytes 2359300
  77.8 117.4 %all-gather.10.cloned.1.call-start = ((), (), s32[]{:S(2)}) async-start(), calls=%async_computation.9 | async-start | bytes 3932160 | tf_op jit(solution)/shard_map/all_gather | solution.py:25
  78.5 215.0 %copy-start.47 = (f32[768]{0:T(1024)}, f32[768]{0:T(1024)S(1)}, u32[]{:S(2)}) copy-start(f32[768]{0:T(1024)S(1)} %get-tuple-element.234) | copy-start | bytes 9220
  149.7 143.8 %copy-start.2 = (f32[4,128,768]{2,1,0:T(8,128)}, f32[4,128,768]{2,1,0:T(8,128)S(1)}, u32[]{:S(2)}) copy-start(f32[4,128,768]{2,1,0:T(8,128)S(1)} %get-tuple-element.357) | copy-start | bytes 4718596
  149.7 143.8 %copy-start.49 = (f32[4,128]{1,0:T(4,128)}, f32[4,128]{1,0:T(4,128)S(1)}, u32[]{:S(2)}) copy-start(f32[4,128]{1,0:T(4,128)S(1)} %broadcast_multiply_fusion.3) | copy-start | bytes 6148
  150.0 51.7 %copy-start.55 = (f32[4,128]{1,0:T(4,128)}, f32[4,128]{1,0:T(4,128)S(1)}, u32[]{:S(2)}) copy-start(f32[4,128]{1,0:T(4,128)S(1)} %multiply_reduce_fusion.11) | copy-start | bytes 6148
  150.1 143.5 %copy-start.51 = (f32[4,128]{1,0:T(4,128)}, f32[4,128]{1,0:T(4,128)S(1)}, u32[]{:S(2)}) copy-start(f32[4,128]{1,0:T(4,128)S(1)} %fusion.160) | copy-start | bytes 6148
  151.3 142.2 %reduce-scatter.11.cloned.1.call-start = ((), (), s32[]{:S(2)}) async-start(), calls=%async_computation.10 | async-start | bytes 7864320 | tf_op jit(solution)/shard_map/reduce_scatter | solution.py:29
  151.6 50.2 %copy-start.59 = (f32[768]{0:T(1024)}, f32[768]{0:T(1024)S(1)}, u32[]{:S(2)}) copy-start(f32[768]{0:T(1024)S(1)} %get-tuple-element.243) | copy-start | bytes 9220
  201.7 15.4 %copy-start.30 = (f32[4,512,768]{2,1,0:T(8,128)}, f32[4,512,768]{2,1,0:T(8,128)S(1)}, u32[]{:S(2)}) copy-start(f32[4,512,768]{2,1,0:T(8,128)S(1)} %get-tuple-element.398) | copy-start | bytes 18874372
  201.8 17.0 %copy-start.75 = (bf16[2,768,768]{2,1,0:T(8,128)(2,1)S(1)}, bf16[2,768,768]{2,1,0:T(8,128)(2,1)}, u32[]{:S(2)}) copy-start(bf16[2,768,768]{2,1,0:T(8,128)(2,1)} %param.38) | copy-start | bytes 7077892
  223.3 119.0 %all-gather.12.cloned.1.call-start = ((), (), s32[]{:S(2)}) async-start(), calls=%async_computation.11 | async-start | bytes 3932160 | tf_op jit(solution)/shard_map/all_gather | solution.py:25
  293.5 3.0 copy-start.37
  295.6 46.8 %copy-start.43 = (bf16[2,3,768,192]{2,3,1,0:T(8,128)(2,1)S(1)}, bf16[2,3,768,192]{2,3,1,0:T(8,128)(2,1)}, u32[]{:S(2)}) copy-start(bf16[2,3,768,192]{2,3,1,0:T(8,128)(2,1)} %param.30) | copy-start | bytes 5308420
  298.4 143.6 %reduce-scatter.13.cloned.1.call-start = ((), (), s32[]{:S(2)}) async-start(), calls=%async_computation.12 | async-start | bytes 7864320 | tf_op jit(solution)/shard_map/reduce_scatter | solution.py:29
  367.0 4.9 copy-start.20
  367.0 4.9 copy-start.25
  371.9 118.9 %all-gather.14.cloned.1.call-start = ((), (), s32[]{:S(2)}) async-start(), calls=%async_computation.13 | async-start | bytes 3932160 | tf_op jit(solution)/shard_map/all_gather | solution.py:25
  446.7 142.2 %reduce-scatter.15.cloned.1.call-start = ((), (), s32[]{:S(2)}) async-start(), calls=%async_computation.14 | async-start | bytes 7864320 | tf_op jit(solution)/shard_map/reduce_scatter | solution.py:29
  497.2 15.4 %copy-start.31 = (f32[4,512,768]{2,1,0:T(8,128)}, f32[4,512,768]{2,1,0:T(8,128)S(1)}, u32[]{:S(2)}) copy-start(f32[4,512,768]{2,1,0:T(8,128)S(1)} %get-tuple-element.399) | copy-start | bytes 18874372
  497.2 17.1 %copy-start.76 = (bf16[2,768,768]{2,1,0:T(8,128)(2,1)S(1)}, bf16[2,768,768]{2,1,0:T(8,128)(2,1)}, u32[]{:S(2)}) copy-start(bf16[2,768,768]{2,1,0:T(8,128)(2,1)} %param.38) | copy-start | bytes 7077892
  518.8 119.2 %all-gather.16.cloned.1.call-start = ((), (), s32[]{:S(2)}) async-start(), calls=%async_computation.15 | async-start | bytes 3932160 | tf_op jit(solution)/shard_map/all_gather | solution.py:25
  594.0 131.7 %reduce-scatter.17.cloned.1.call-start = ((), (), s32[]{:S(2)}) async-start(), calls=%async_computation.16 | async-start | bytes 7864320 | tf_op jit(solution)/shard_map/reduce_scatter | solution.py:29
  638.0 12.9 copy-start.77
  655.4 122.3 %all-gather.18.cloned.1.call-start = ((), (), s32[]{:S(2)}) async-start(), calls=%async_computation.17 | async-start | bytes 3932160 | tf_op jit(solution)/shard_map/all_gather | solution.py:25
  730.9 46.9 %copy-start.44 = (bf16[2,192,768]{2,1,0:T(8,128)(2,1)S(1)}, bf16[2,192,768]{2,1,0:T(8,128)(2,1)}, u32[]{:S(2)}) copy-start(bf16[2,192,768]{2,1,0:T(8,128)(2,1)} %param.32) | copy-start | bytes 1769476
  733.7 177.3 %reduce-scatter.19.cloned.1.call-start = ((), (), s32[]{:S(2)}) async-start(), calls=%async_computation.18 | async-start | bytes 7864320 | tf_op jit(solution)/shard_map/reduce_scatter | solution.py:29
  818.8 4.8 copy-start.9
  828.3 75.6 %copy-start.70 = (s32[64]{0:T(128)S(1)}, s32[64]{0:T(128)}, u32[]{:S(2)}) copy-start(s32[64]{0:T(128)} %param.29) | copy-start | bytes 772
  828.4 132.0 %all-gather.20.cloned.1.call-start = ((), (), s32[]{:S(2)}) async-start(), calls=%async_computation.19 | async-start | bytes 3932160 | tf_op jit(solution)/shard_map/all_gather | solution.py:25
  828.4 82.6 %copy-start.6 = (f32[4,128,768]{2,1,0:T(8,128)S(1)}, f32[4,128,768]{2,1,0:T(8,128)}, u32[]{:S(2)}) copy-start(f32[4,128,768]{2,1,0:T(8,128)} %copy-done.5) | copy-start | bytes 4718596
  906.3 8.3 copy-start.58
  914.6 45.7 %copy-start.60 = (f32[768]{0:T(1024)S(1)}, f32[768]{0:T(1024)}, u32[]{:S(2)}) copy-start(f32[768]{0:T(1024)} %copy-done.59) | copy-start | bytes 9220
  916.3 131.0 %reduce-scatter.21.cloned.1.call-start = ((), (), s32[]{:S(2)}) async-start(), calls=%async_computation.20 | async-start | bytes 7864320 | tf_op jit(solution)/shard_map/reduce_scatter | solution.py:29
  960.3 12.3 copy-start.78
  977.2 70.2 %copy-start.3 = (f32[4,128,768]{2,1,0:T(8,128)S(1)}, f32[4,128,768]{2,1,0:T(8,128)}, u32[]{:S(2)}) copy-start(f32[4,128,768]{2,1,0:T(8,128)} %copy-done.2) | copy-start | bytes 4718596
  977.2 70.2 %copy-start.48 = (f32[768]{0:T(1024)S(1)}, f32[768]{0:T(1024)}, u32[]{:S(2)}) copy-start(f32[768]{0:T(1024)} %copy-done.47) | copy-start | bytes 9220
  977.2 70.2 %copy-start.50 = (f32[4,128]{1,0:T(4,128)S(1)}, f32[4,128]{1,0:T(4,128)}, u32[]{:S(2)}) copy-start(f32[4,128]{1,0:T(4,128)} %copy-done.49) | copy-start | bytes 6148
  977.2 70.2 %copy-start.52 = (f32[4,128]{1,0:T(4,128)S(1)}, f32[4,128]{1,0:T(4,128)}, u32[]{:S(2)}) copy-start(f32[4,128]{1,0:T(4,128)} %copy-done.51) | copy-start | bytes 6148
  977.2 72.4 %copy-start.56 = (f32[4,128]{1,0:T(4,128)S(1)}, f32[4,128]{1,0:T(4,128)}, u32[]{:S(2)}) copy-start(f32[4,128]{1,0:T(4,128)} %copy-done.55) | copy-start | bytes 6148
  977.2 119.3 %all-gather.22.cloned.1.call-start = ((), (), s32[]{:S(2)}) async-start(), calls=%async_computation.21 | async-start | bytes 3932160 | tf_op jit(solution)/shard_map/all_gather | solution.py:25
  1052.5 387.3 %all-reduce.5.cloned.1.call-start = ((), (), s32[]{:S(2)}) async-start(), calls=%async_computation.24 | async-start | bytes 28311552 | tf_op jit(solution)/shard_map/psum | solution.py:354
  1053.0 6.1 copy-start.73
  1053.0 6.1 copy-start.80
  1059.1 4.2 copy-start.1
  1059.1 4.2 copy-start.10
  1068.5 3.1 copy-start.74
  1071.5 4.2 copy-start.72
  1071.5 4.2 copy-start.82
  1075.7 20.8 %copy-start.45 = (bf16[2,192,768]{2,1,0:T(8,128)(2,1)S(1)}, bf16[2,192,768]{2,1,0:T(8,128)(2,1)}, u32[]{:S(2)}) copy-start(bf16[2,192,768]{2,1,0:T(8,128)(2,1)} %param.32) | copy-start | bytes 1769476
  1103.3 41.8 %copy-start = (bf16[1,4,512,768]{3,2,1,0:T(8,128)(2,1)S(1)}, bf16[1,4,512,768]{3,2,1,0:T(8,128)(2,1)}, u32[]{:S(2)}) copy-start(bf16[1,4,512,768]{3,2,1,0:T(8,128)(2,1)} %all-gather.24.cloned.1.call-done) | copy-start | bytes 9437188
  1153.5 359.3 %reduce-scatter.23.cloned.1.call-start = ((), (), s32[]{:S(2)}) async-start(), calls=%async_computation.22 | async-start | bytes 7864320 | tf_op jit(solution)/shard_map/reduce_scatter | solution.py:29
  1163.8 3.8 copy-start.7
  1442.2 3.7 copy-start.40
  1442.2 3.7 copy-start.41
  1445.9 4.5 copy-start.39
  1450.5 62.4 %copy-start.15 = (f32[4,128,768]{2,1,0:T(8,128)S(1)}, f32[4,128,768]{2,1,0:T(8,128)}, u32[]{:S(2)}) copy-start(f32[4,128,768]{2,1,0:T(8,128)} %copy-done.14) | copy-start | bytes 4718596
  (36 other events, 64.6 us)
Sparse Core Ops, SparseCore 0:
  9.8 46.5 all-gather.23
  78.0 70.0 reduce-scatter.8
  151.4 43.8 all-gather.9
  223.5 70.0 reduce-scatter.10
  298.5 43.8 all-gather.11
  372.0 70.0 reduce-scatter.12
  446.8 43.8 all-gather.13
  518.9 70.0 reduce-scatter.14
  594.1 43.8 all-gather.15
  655.5 70.0 reduce-scatter.16
  733.9 43.8 all-gather.17
  828.5 82.5 reduce-scatter.18
  916.5 43.8 all-gather.19
  977.3 70.0 reduce-scatter.20
  1052.6 43.8 all-gather.21
  1153.6 286.0 all-reduce.4
  1442.6 70.1 reduce-scatter.22
where the time goes:
time: 1530 us; the launch traced here: 1520 us
  waiting for transfers between devices  1000 us (65%)
  matrix products  173 us (11%)
  blocking collectives  145 us (9%)
  other arithmetic  109 us (7%)
  local copies, waits for them, and re-layouts  72 us (5%)
  between operations  18.6 us (1%)
    reduce_scatter x8, waiting for transfers between devices, collect_rows(): return lax.psum_scatter(values, 'tensor', scatter_dimension=1, tiled=True)  484 us
    all_gather x8, waiting for transfers between devices, spread_rows(): return lax.all_gather(values, 'tensor', axis=1, tiled=True)  324 us
    psum x1, waiting for transfers between devices, shards(): lax.psum((backbone_matrices[0], backbone_matrices[1], backbone_matrices[2...  194 us
    all_gather x1, blocking collectives, shards(): lax.all_gather(chosen.reshape(slot_count, feature_count).astype(jnp.bfloa...  74 us
    psum x1, blocking collectives, shards(): lax.psum((backbone_vectors[0], backbone_vectors[1], backbone_vectors[2],...  41.6 us
    dynamic_slice x64, local copies, waits for them, and re-layouts, layer_forward(): lax.map(attend_forward, (queries, key_rows, value_rows, segment))  38.4 us
    convert_element_type x2, other arithmetic, layer_forward(): activated = activate(expanded).astype(jnp.bfloat16)  30.8 us
  transfers between devices with their start and end apart: 17, of which 17 were waited for; matrix products, arithmetic and copies ran while one was open for 4% of the time, Pallas kernels for 0%

commit v1 on v0

--- a/solution.py
+++ b/solution.py
@@ -1,3 +1,4 @@
+import functools
 import math
 import jax
 import jax.numpy as jnp
@@ -11,6 +12,31 @@
 MASKED = -1e30
 
 
+def place_slots(local_array, bus_axis):
+    v1 = jax.lax.axis_size(bus_axis)
+    taken_in, current_arr, z1 = (v1, jax.lax.axis_index(bus_axis), local_array.shape[1])
+    series = [(i, (i + 1) % taken_in) for i in range(taken_in)]
+    seen = [(i, (i - 1) % taken_in) for i in range(taken_in)]
+    val = jnp.zeros(
+        (*local_array.shape[:1], taken_in * z1, *local_array.shape[2:]), local_array.dtype
+    )
+    val = lax.dynamic_update_slice_in_dim(val, local_array, current_arr * z1, axis=1)
+    x_new = placed = local_array
+    part_now = taken_in // 2
+    for h in range(1, part_now + 1):
+        x_new = jax.lax.ppermute(x_new, bus_axis, series)
+        val = lax.dynamic_update_slice_in_dim(val, x_new, (current_arr - h) % taken_in * z1, axis=1)
+        if h < taken_in - part_now:
+            placed = jax.lax.ppermute(placed, bus_axis, seen)
+            val = lax.dynamic_update_slice_in_dim(
+                val, placed, (current_arr + h) % taken_in * z1, axis=1
+            )
+    return val
+
+
+_try_all_cube = functools.partial(place_slots, bus_axis="tensor")
+
+
 def normalize(values, norm_scale, norm_offset):
     centred = values - jnp.mean(values, axis=-1, keepdims=True)
     spread = jnp.mean(centred * centred, axis=-1, keepdims=True)
@@ -22,7 +48,7 @@
 
 
 def spread_rows(values):
-    return lax.all_gather(values, "tensor", axis=1, tiled=True)
+    return _try_all_cube(values)
 
 
 def collect_rows(values):

time: 1530 us -> 1630 us (1.065)
  waiting for transfers between devices: 1000 us -> 1090 us
  starting transfers between devices: 2.59 us -> 31.4 us
    ppermute x0 -> x24, waiting for transfers between devices: none -> 383 us  [the longest x16 262 us: place_slots(): x_new = jax.lax.ppermute(x_new, bus_axis, series)]
    all_gather x8 -> x0, waiting for transfers between devices: 324 us -> none  [spread_rows(): return lax.all_gather(values, 'tensor', axis=1, tiled=True)]
    psum x1, waiting for transfers between devices: 194 us -> 236 us  [shards(): lax.psum((backbone_matrices[0], backbone_matrices[1], backbone_matrices[2...]
    ppermute x0 -> x24, starting transfers between devices: none -> 30.5 us  [the longest x16 18.6 us: place_slots(): x_new = jax.lax.ppermute(x_new, bus_axis, series)]
    reduce_scatter x8, waiting for transfers between devices: 484 us -> 467 us  [collect_rows(): return lax.psum_scatter(values, 'tensor', scatter_dimension=1, tiled=True)]
  transfers between devices with their start and end apart: 17 -> 33, of which waited for: 17 -> 33; matrix products, arithmetic and copies ran while one was open for 4% -> 4% of each run, Pallas kernels for 0% -> 0%
where the time goes in v1:
time: 1630 us; the launch traced here: 1620 us
  waiting for transfers between devices  1090 us (67%)
  matrix products  160 us (10%)
  blocking collectives  140 us (9%)
  other arithmetic  103 us (6%)
  local copies, waits for them, and re-layouts  78.1 us (5%)
  starting transfers between devices  31.4 us (2%)
  between operations  19.1 us (1%)
    reduce_scatter x8, waiting for transfers between devices, collect_rows(): return lax.psum_scatter(values, 'tensor', scatter_dimension=1, tiled=True)  467 us
    ppermute x16, waiting for transfers between devices, place_slots(): x_new = jax.lax.ppermute(x_new, bus_axis, series)  262 us
    psum x1, waiting for transfers between devices, shards(): lax.psum((backbone_matrices[0], backbone_matrices[1], backbone_matrices[2...  236 us
    ppermute x8, waiting for transfers between devices, place_slots(): placed = jax.lax.ppermute(placed, bus_axis, seen)  121 us
    all_gather x1, blocking collectives, shards(): lax.all_gather(chosen.reshape(slot_count, feature_count).astype(jnp.bfloa...  70.6 us
    psum x1, blocking collectives, shards(): lax.psum((backbone_vectors[0], backbone_vectors[1], backbone_vectors[2],...  40 us
    dynamic_slice x64, local copies, waits for them, and re-layouts, layer_forward(): lax.map(attend_forward, (queries, key_rows, value_rows, segment))  34.8 us
  transfers between devices with their start and end apart: 33, of which 33 were waited for; matrix products, arithmetic and copies ran while one was open for 4% of the time, Pallas kernels for 0%

profile of v1, /device:TPU:0, one launch (start us, length us, event | category | flops | bytes accessed | tf_op | source)
XLA Modules:
  0.0 1619.5 jit_solution(9411621736425316578)
XLA Ops:
  13.6 16.2 %collective-permute-done = bf16[4,128,768]{2,1,0:T(8,128)(2,1)S(1)} collective-permute-done((bf16[4,128,768]{2,1,0:T(8,128)(2,1)}, bf16[4,128,768]{2,1,0:T(8,128)(2,1)S(1)}, u32[]{:S(2)}, u32[]{:S(2)}) %collective-permute-start) | collective-permute-done | bytes 786464 | tf_op jit(solution)/shard_map/ppermute | solution.py:27
  32.3 14.9 collective-permute-done.1
  47.3 15.4 collective-permute-done.2
  65.2 11.7 while.52
  77.0 4.9 fusion.124
  82.8 70.0 %reduce-scatter.9.cloned.1.call-done = f32[4,128,768]{2,1,0:T(8,128)} async-done(((f32[4,512,768]{2,1,0:T(8,128)}), f32[4,128,768]{2,1,0:T(8,128)}) %reduce-scatter.9.cloned.1.call-update) | async-done | bytes 1572880 | tf_op jit(solution)/shard_map/reduce_scatter | solution.py:55
  158.5 18.4 %collective-permute-done.3 = bf16[4,128,768]{2,1,0:T(8,128)(2,1)S(1)} collective-permute-done((bf16[4,128,768]{2,1,0:T(8,128)(2,1)S(1)}, bf16[4,128,768]{2,1,0:T(8,128)(2,1)S(1)}, u32[]{:S(2)}, u32[]{:S(2)}) %collective-permute-start.3) | collective-permute-done | bytes 786464 | tf_op jit(solution)/shard_map/ppermute | solution.py:27
  178.0 15.7 collective-permute-done.4
  193.8 15.5 collective-permute-done.5
  209.3 4.1 fusion.73
  213.5 15.4 multiply_convert_fusion.3
  230.6 4.5 fusion.84
  236.0 69.4 %reduce-scatter.11.cloned.1.call-done = f32[4,128,768]{2,1,0:T(8,128)} async-done(((f32[4,512,768]{2,1,0:T(8,128)}), f32[4,128,768]{2,1,0:T(8,128)}) %reduce-scatter.11.cloned.1.call-update) | async-done | bytes 1572880 | tf_op jit(solution)/shard_map/reduce_scatter | solution.py:55
  313.9 18.7 %collective-permute-done.6 = bf16[4,128,768]{2,1,0:T(8,128)(2,1)} collective-permute-done((bf16[4,128,768]{2,1,0:T(8,128)(2,1)}, bf16[4,128,768]{2,1,0:T(8,128)(2,1)}, u32[]{:S(2)}, u32[]{:S(2)}) %collective-permute-start.6) | collective-permute-done | bytes 786464 | tf_op jit(solution)/shard_map/ppermute | solution.py:27
  334.6 14.8 collective-permute-done.7
  350.6 14.4 collective-permute-done.8
  369.5 15.5 while.53
  385.1 3.7 fusion.121
  388.9 70.1 %reduce-scatter.13.cloned.1.call-done = f32[4,128,768]{2,1,0:T(8,128)} async-done(((f32[4,512,768]{2,1,0:T(8,128)}), f32[4,128,768]{2,1,0:T(8,128)}) %reduce-scatter.13.cloned.1.call-update) | async-done | bytes 1572880 | tf_op jit(solution)/shard_map/reduce_scatter | solution.py:55
  459.0 3.1 fusion.158
  466.0 18.4 %collective-permute-done.9 = bf16[4,128,768]{2,1,0:T(8,128)(2,1)S(1)} collective-permute-done((bf16[4,128,768]{2,1,0:T(8,128)(2,1)S(1)}, bf16[4,128,768]{2,1,0:T(8,128)(2,1)S(1)}, u32[]{:S(2)}, u32[]{:S(2)}) %collective-permute-start.9) | collective-permute-done | bytes 786464 | tf_op jit(solution)/shard_map/ppermute | solution.py:27
  485.3 15.9 collective-permute-done.10
  501.3 15.5 collective-permute-done.11
  516.8 4.1 fusion.74
  521.0 15.4 multiply_convert_fusion.2
  538.1 4.5 fusion.78
  542.6 70.1 %reduce-scatter.15.cloned.1.call-done = f32[4,128,768]{2,1,0:T(8,128)} async-done(((f32[4,512,768]{2,1,0:T(8,128)}), f32[4,128,768]{2,1,0:T(8,128)}) %reduce-scatter.15.cloned.1.call-update) | async-done | bytes 1572880 | tf_op jit(solution)/shard_map/reduce_scatter | solution.py:55
  620.1 18.4 %collective-permute-done.12 = bf16[4,128,768]{2,1,0:T(8,128)(2,1)S(1)} collective-permute-done((bf16[4,128,768]{2,1,0:T(8,128)(2,1)S(1)}, bf16[4,128,768]{2,1,0:T(8,128)(2,1)S(1)}, u32[]{:S(2)}, u32[]{:S(2)}) %collective-permute-start.12) | collective-permute-done | bytes 786464 | tf_op jit(solution)/shard_map/ppermute | solution.py:27
  639.2 16.1 collective-permute-done.13
  655.4 15.5 collective-permute-done.14
  671.0 9.4 fusion.165
  682.1 4.5 fusion.69
  686.8 70.1 %reduce-scatter.17.cloned.1.call-done = f32[4,128,768]{2,1,0:T(8,128)} async-done(((f32[4,512,768]{2,1,0:T(8,128)}), f32[4,128,768]{2,1,0:T(8,128)}) %reduce-scatter.17.cloned.1.call-update) | async-done | bytes 1572880 | tf_op jit(solution)/shard_map/reduce_scatter | solution.py:55
  756.9 4.6 add_reduce_fusion.3
  768.4 18.6 %collective-permute-done.15 = bf16[4,128,768]{2,1,0:T(8,128)(2,1)S(1)} collective-permute-done((bf16[4,128,768]{2,1,0:T(8,128)(2,1)}, bf16[4,128,768]{2,1,0:T(8,128)(2,1)S(1)}, u32[]{:S(2)}, u32[]{:S(2)}) %collective-permute-start.15) | collective-permute-done | bytes 786464 | tf_op jit(solution)/shard_map/ppermute | solution.py:27
  788.5 15.3 collective-permute-done.16
  804.8 14.7 collective-permute-done.17
  821.6 4.0 convolution_convert_fusion.1
  826.6 36.0 %while.54 = (s32[]{:T(128)}, bf16[4,512,192]{1,2,0:T(8,128)(2,1)S(1)}, bf16[4,512,192]{1,2,0:T(8,128)(2,1)}, bf16[4,512,192]{1,2,0:T(8,128)(2,1)S(1)}, bf16[4,51...) while((s32[]{:T(128)}, ...), condition=%wide.region_39.40_spmd, body=%wide.region_37.39_spmd.sunk | while | flops 511146496 | bytes 28873352 | solution.py:223
  867.5 4.7 add_add_fusion.1
  873.8 70.6 %all_gather.3 = bf16[512,768]{1,0:T(8,128)(2,1)S(1)} all-gather(bf16[16,768]{1,0:T(8,128)(2,1)S(1)} %convert_element_type.392), channel_id=1, replica_groups=mesh['dp'=4,'span'=2,'tensor'=4] {'dp','span','tensor'}, dimensions={0}, use_global_device_ids=true | all-gather | bytes 811008 | tf_op jit(solution)/shard_map/all_gather | solution.py:318
  947.3 7.7 reduce-scatter.19.cloned.1.call-done
  955.0 3.6 multiply_reduce_fusion.3
  962.7 18.4 %collective-permute-done.18 = bf16[4,128,768]{2,1,0:T(8,128)(2,1)S(1)} collective-permute-done((bf16[4,128,768]{2,1,0:T(8,128)(2,1)S(1)}, bf16[4,128,768]{2,1,0:T(8,128)(2,1)S(1)}, u32[]{:S(2)}, u32[]{:S(2)}) %collective-permute-start.18) | collective-permute-done | bytes 786464 | tf_op jit(solution)/shard_map/ppermute | solution.py:27
  981.1 16.8 %collective-permute-done.19 = bf16[4,128,768]{2,1,0:T(8,128)(2,1)S(1)} collective-permute-done((bf16[4,128,768]{2,1,0:T(8,128)(2,1)S(1)}, bf16[4,128,768]{2,1,0:T(8,128)(2,1)S(1)}, u32[]{:S(2)}, u32[]{:S(2)}) %collective-permute-start.19) | collective-permute-done | bytes 786464 | tf_op jit(solution)/shard_map/ppermute | solution.py:30
  998.0 15.5 collective-permute-done.20
  1013.6 5.8 fusion.166
  1021.1 4.5 fusion.66
  1026.2 7.2 convolution_bitcast_fusion
  1033.4 4.1 convolution_bitcast_fusion.2
  1037.6 3.7 convolution_bitcast_fusion.10
  1046.1 49.9 %reduce-scatter.21.cloned.1.call-done = f32[4,128,768]{2,1,0:T(8,128)} async-done(((f32[4,512,768]{2,1,0:T(8,128)}), f32[4,128,768]{2,1,0:T(8,128)}) %reduce-scatter.21.cloned.1.call-update) | async-done | bytes 1572880 | tf_op jit(solution)/shard_map/reduce_scatter | solution.py:55
  1103.4 4.2 convolution_bitcast_fusion.1
  1109.0 12.5 collective-permute-done.21
  1122.2 4.2 convolution_bitcast_fusion.3
  1126.5 11.8 collective-permute-done.22
  1138.4 15.5 collective-permute-done.23
  1160.5 41.8 %while.55 = (s32[]{:T(128)}, bf16[4,512,192]{1,2,0:T(8,128)(2,1)}, bf16[4,512,192]{1,2,0:T(8,128)(2,1)}, bf16[4,512,192]{1,2,0:T(8,128)(2,1)}, bf16[4,512,192]{1...) while((s32[]{:T(128)}, bf16[4,512,192]{1,2,0:T(8,128)(2,1)}, ...), condition=%wide.region_48.49_spmd, body=%wide.region_46.48_spmd.sunk | while | flops 511146496 | bytes 28873860 | solution.py:223
  1213.7 4.8 add_add_fusion
  1226.7 29.2 %all-reduce.1 = (f32[1,2,192]{2,1,0:T(2,128)S(1)}, f32[1,2,192]{2,1,0:T(2,128)S(1)}, f32[1,768]{1,0:T(1,128)S(1)}, f32[1,768]{1,0:T(1,128)S(1)}) all-reduce(f32[1,2,192]{2,1,0:T(2,128)S(1)} %maximum_bitcast_fusion.7, f32[1,2,192]{2,1,0:T(2,128)S(1)} %maximum_bitcast_fusion.6, ...), channel_id=1, replica_groups=mesh['dp'=4,'span'=2,'tensor'=4] {'dp','span'}, use_global_device_ids=true, to_apply=%region_57.58 | all-reduce | flops 2304 | bytes 18432 | tf_op jit(solution)/shard_map/psum | solution.py:380
  1257.0 236.4 %all-reduce.5.cloned.1.call-done = (f32[1,3,768,192]{2,3,1,0:T(8,128)}, f32[1,3,768,192]{2,3,1,0:T(8,128)}, f32[1,192,768]{2,1,0:T(8,128)}, f32[1,192,768]{2,1,0...) async-done(((f32[1,3,768,192]{2,3,1,0:T(8,128)}, f32[1,3,768,192]{2,3,1,0:T(8,128)}, ...) | async-done | bytes 14155792 | tf_op jit(solution)/shard_map/psum | solution.py:380
  1495.9 3.7 pad_maximum_fusion.2
  1506.6 60.0 %reduce-scatter.23.cloned.1.call-done = f32[4,128,768]{2,1,0:T(8,128)} async-done(((f32[4,512,768]{2,1,0:T(8,128)}), f32[4,128,768]{2,1,0:T(8,128)}) %reduce-scatter.23.cloned.1.call-update) | async-done | bytes 1572880 | tf_op jit(solution)/shard_map/reduce_scatter | solution.py:55
  1569.2 40.0 %all-reduce = (f32[1,768]{1,0:T(1,128)S(1)}, f32[1,768]{1,0:T(1,128)S(1)}, f32[1,2,768]{2,1,0:T(2,128)S(1)}, f32[1,2,768]{2,1,0:T(2,128)S(1)}, f32[1,2,768]{2,1,...) all-reduce(f32[1,768]{1,0:T(1,128)S(1)} %stack.204, ...), channel_id=1, replica_groups=mesh['dp'=4,'span'=2,'tensor'=4] {'dp','span','tensor'}, use_global_device_ids=true, to_apply=%region_63.64 | all-reduce | flops 9216 | bytes 73728 | tf_op jit(solution)/shard_map/psum | solution.py:399
  (607 shorter events, 240.2 us)
Async XLA Ops:
  7.2 145.6 %reduce-scatter.9.cloned.1.call-start = ((), (), s32[]{:S(2)}) async-start(), calls=%async_computation.8 | async-start | bytes 7864320 | tf_op jit(solution)/shard_map/reduce_scatter | solution.py:55
  7.2 22.6 %collective-permute-start = (bf16[4,128,768]{2,1,0:T(8,128)(2,1)}, bf16[4,128,768]{2,1,0:T(8,128)(2,1)S(1)}, u32[]{:S(2)}, u32[]{:S(2)}) collective-permute-start(bf16[4,128,768]{2,1,0:T(8,128)(2,1)} %bitcast.500), channel_id=1, source_target_pairs={{0,1},{1,2},{2,3},{3,0},{4,5},{5,6},{6,7},{7,4},{8,9},{9,10},{10,1... | collective-permute-start | bytes 2359304 | tf_op jit(solution)/shard_map/ppermute | solution.py:27
  10.3 36.9 %collective-permute-start.1 = (bf16[4,128,768]{2,1,0:T(8,128)(2,1)}, bf16[4,128,768]{2,1,0:T(8,128)(2,1)S(1)}, u32[]{:S(2)}, u32[]{:S(2)}) collective-permute-start(bf16[4,128,768]{2,1,0:T(8,128)(2,1)} %bitcast.501), channel_id=1, source_target_pairs={{0,3},{1,0},{2,1},{3,2},{4,7},{5,4},{6,5},{7,6},{8,11},{9,8},{10,9... | collective-permute-start | bytes 2359304 | tf_op jit(solution)/shard_map/ppermute | solution.py:30
  12.8 223.0 %copy-start.66 = (s32[4,4]{1,0:T(4,128)}, s32[4,4]{1,0:T(4,128)S(1)}, u32[]{:S(2)}) copy-start(s32[4,4]{1,0:T(4,128)S(1)} %bitcast_subtract_fusion) | copy-start | bytes 196
  29.8 32.9 %collective-permute-start.2 = (bf16[4,128,768]{2,1,0:T(8,128)(2,1)S(1)}, bf16[4,128,768]{2,1,0:T(8,128)(2,1)S(1)}, u32[]{:S(2)}, u32[]{:S(2)}) collective-permute-start(bf16[4,128,768]{2,1,0:T(8,128)(2,1)S(1)} %collective-permute-done), channel_id=1, source_target_pairs={{0,1},{1,2},{2,3},{3,0},{4,5},{5,6},{6,7},{7,4},{8,9},{9,10},{10,1... | collective-permute-start | bytes 2359304 | tf_op jit(solution)/shard_map/ppermute | solution.py:27
  32.1 30.6 %copy-start.56 = (bf16[2,3,768,192]{2,3,1,0:T(8,128)(2,1)S(1)}, bf16[2,3,768,192]{2,3,1,0:T(8,128)(2,1)}, u32[]{:S(2)}) copy-start(bf16[2,3,768,192]{2,3,1,0:T(8,128)(2,1)} %param.30) | copy-start | bytes 5308420
  82.0 70.8 %copy-start.46 = (bf16[1,4,128,768]{3,2,1,0:T(8,128)(2,1)S(1)}, bf16[1,4,128,768]{3,2,1,0:T(8,128)(2,1)}, u32[]{:S(2)}) copy-start(bf16[1,4,128,768]{3,2,1,0:T(8,128)(2,1)} %param.24) | copy-start | bytes 2359300
  82.0 223.3 %reduce-scatter.11.cloned.1.call-start = ((), (), s32[]{:S(2)}) async-start(), calls=%async_computation.9 | async-start | bytes 7864320 | tf_op jit(solution)/shard_map/reduce_scatter | solution.py:55
  82.7 222.6 %copy-start.62 = (f32[768]{0:T(1024)}, f32[768]{0:T(1024)S(1)}, u32[]{:S(2)}) copy-start(f32[768]{0:T(1024)S(1)} %get-tuple-element.234) | copy-start | bytes 9220
  154.4 150.9 %copy-start.6 = (f32[4,128,768]{2,1,0:T(8,128)}, f32[4,128,768]{2,1,0:T(8,128)S(1)}, u32[]{:S(2)}) copy-start(f32[4,128,768]{2,1,0:T(8,128)S(1)} %get-tuple-element.371) | copy-start | bytes 4718596
  154.5 150.9 %copy-start.64 = (f32[4,128]{1,0:T(4,128)}, f32[4,128]{1,0:T(4,128)S(1)}, u32[]{:S(2)}) copy-start(f32[4,128]{1,0:T(4,128)S(1)} %broadcast_multiply_fusion.3) | copy-start | bytes 6148
  154.8 150.6 %copy-start.68 = (f32[4,128]{1,0:T(4,128)}, f32[4,128]{1,0:T(4,128)S(1)}, u32[]{:S(2)}) copy-start(f32[4,128]{1,0:T(4,128)S(1)} %fusion.144) | copy-start | bytes 6148
  155.5 53.8 %copy-start.92 = (bf16[2,768,768]{2,1,0:T(8,128)(2,1)S(1)}, bf16[2,768,768]{2,1,0:T(8,128)(2,1)}, u32[]{:S(2)}) copy-start(bf16[2,768,768]{2,1,0:T(8,128)(2,1)} %param.36) | copy-start | bytes 7077892
  155.5 21.3 %collective-permute-start.3 = (bf16[4,128,768]{2,1,0:T(8,128)(2,1)S(1)}, bf16[4,128,768]{2,1,0:T(8,128)(2,1)S(1)}, u32[]{:S(2)}, u32[]{:S(2)}) collective-permute-start(bf16[4,128,768]{2,1,0:T(8,128)(2,1)S(1)} %get-tuple-element.369), channel_id=1, source_target_pairs={{0,1},{1,2},{2,3},{3,0},{4,5},{5,6},{6,7},{7,4},{8,9},{9,10},{10,1... | collective-permute-start | bytes 2359304 | tf_op jit(solution)/shard_map/ppermute | solution.py:27
  157.0 36.7 %collective-permute-start.4 = (bf16[4,128,768]{2,1,0:T(8,128)(2,1)S(1)}, bf16[4,128,768]{2,1,0:T(8,128)(2,1)S(1)}, u32[]{:S(2)}, u32[]{:S(2)}) collective-permute-start(bf16[4,128,768]{2,1,0:T(8,128)(2,1)S(1)} %get-tuple-element.369), channel_id=1, source_target_pairs={{0,3},{1,0},{2,1},{3,2},{4,7},{5,4},{6,5},{7,6},{8,11},{9,8},{10,9... | collective-permute-start | bytes 2359304 | tf_op jit(solution)/shard_map/ppermute | solution.py:30
  176.8 32.4 %collective-permute-start.5 = (bf16[4,128,768]{2,1,0:T(8,128)(2,1)S(1)}, bf16[4,128,768]{2,1,0:T(8,128)(2,1)S(1)}, u32[]{:S(2)}, u32[]{:S(2)}) collective-permute-start(bf16[4,128,768]{2,1,0:T(8,128)(2,1)S(1)} %collective-permute-done.3), channel_id=1, source_target_pairs={{0,1},{1,2},{2,3},{3,0},{4,5},{5,6},{6,7},{7,4},{8,9},{9,10},{10,1... | collective-permute-start | bytes 2359304 | tf_op jit(solution)/shard_map/ppermute | solution.py:27
  177.9 35.5 %copy-start.76 = (f32[768]{0:T(1024)}, f32[768]{0:T(1024)S(1)}, u32[]{:S(2)}) copy-start(f32[768]{0:T(1024)S(1)} %get-tuple-element.243) | copy-start | bytes 9220
  235.2 223.8 %reduce-scatter.13.cloned.1.call-start = ((), (), s32[]{:S(2)}) async-start(), calls=%async_computation.10 | async-start | bytes 7864320 | tf_op jit(solution)/shard_map/reduce_scatter | solution.py:55
  310.9 21.6 %collective-permute-start.6 = (bf16[4,128,768]{2,1,0:T(8,128)(2,1)}, bf16[4,128,768]{2,1,0:T(8,128)(2,1)}, u32[]{:S(2)}, u32[]{:S(2)}) collective-permute-start(bf16[4,128,768]{2,1,0:T(8,128)(2,1)} %get-tuple-element.363), channel_id=1, source_target_pairs={{0,1},{1,2},{2,3},{3,0},{4,5},{5,6},{6,7},{7,4},{8,9},{9,10},{10,1... | collective-permute-start | bytes 2359304 | tf_op jit(solution)/shard_map/ppermute | solution.py:27
  312.4 37.0 %collective-permute-start.7 = (bf16[4,128,768]{2,1,0:T(8,128)(2,1)}, bf16[4,128,768]{2,1,0:T(8,128)(2,1)}, u32[]{:S(2)}, u32[]{:S(2)}) collective-permute-start(bf16[4,128,768]{2,1,0:T(8,128)(2,1)} %get-tuple-element.363), channel_id=1, source_target_pairs={{0,3},{1,0},{2,1},{3,2},{4,7},{5,4},{6,5},{7,6},{8,11},{9,8},{10,9... | collective-permute-start | bytes 2359304 | tf_op jit(solution)/shard_map/ppermute | solution.py:30
  332.6 32.4 %collective-permute-start.8 = (bf16[4,128,768]{2,1,0:T(8,128)(2,1)}, bf16[4,128,768]{2,1,0:T(8,128)(2,1)}, u32[]{:S(2)}, u32[]{:S(2)}) collective-permute-start(bf16[4,128,768]{2,1,0:T(8,128)(2,1)} %collective-permute-done.6), channel_id=1, source_target_pairs={{0,1},{1,2},{2,3},{3,0},{4,5},{5,6},{6,7},{7,4},{8,9},{9,10},{10,1... | collective-permute-start | bytes 2359304 | tf_op jit(solution)/shard_map/ppermute | solution.py:27
  333.3 32.9 %copy-start.57 = (bf16[2,3,768,192]{2,3,1,0:T(8,128)(2,1)S(1)}, bf16[2,3,768,192]{2,3,1,0:T(8,128)(2,1)}, u32[]{:S(2)}) copy-start(bf16[2,3,768,192]{2,3,1,0:T(8,128)(2,1)} %param.30) | copy-start | bytes 5308420
  388.7 70.2 %copy-start.5 = (f32[4,128,768]{2,1,0:T(8,128)S(1)}, f32[4,128,768]{2,1,0:T(8,128)}, u32[]{:S(2)}) copy-start(f32[4,128,768]{2,1,0:T(8,128)} %copy-done.4) | copy-start | bytes 4718596
  388.8 224.0 %reduce-scatter.15.cloned.1.call-start = ((), (), s32[]{:S(2)}) async-start(), calls=%async_computation.11 | async-start | bytes 7864320 | tf_op jit(solution)/shard_map/reduce_scatter | solution.py:55
  463.0 53.9 %copy-start.93 = (bf16[2,768,768]{2,1,0:T(8,128)(2,1)S(1)}, bf16[2,768,768]{2,1,0:T(8,128)(2,1)}, u32[]{:S(2)}) copy-start(bf16[2,768,768]{2,1,0:T(8,128)(2,1)} %param.36) | copy-start | bytes 7077892
  463.0 21.4 %collective-permute-start.9 = (bf16[4,128,768]{2,1,0:T(8,128)(2,1)S(1)}, bf16[4,128,768]{2,1,0:T(8,128)(2,1)S(1)}, u32[]{:S(2)}, u32[]{:S(2)}) collective-permute-start(bf16[4,128,768]{2,1,0:T(8,128)(2,1)S(1)} %get-tuple-element.359), channel_id=1, source_target_pairs={{0,1},{1,2},{2,3},{3,0},{4,5},{5,6},{6,7},{7,4},{8,9},{9,10},{10,1... | collective-permute-start | bytes 2359304 | tf_op jit(solution)/shard_map/ppermute | solution.py:27
  464.5 36.7 %collective-permute-start.10 = (bf16[4,128,768]{2,1,0:T(8,128)(2,1)S(1)}, bf16[4,128,768]{2,1,0:T(8,128)(2,1)S(1)}, u32[]{:S(2)}, u32[]{:S(2)}) collective-permute-start(bf16[4,128,768]{2,1,0:T(8,128)(2,1)S(1)} %get-tuple-element.359), channel_id=1, source_target_pairs={{0,3},{1,0},{2,1},{3,2},{4,7},{5,4},{6,5},{7,6},{8,11},{9,8},{10,9... | collective-permute-start | bytes 2359304 | tf_op jit(solution)/shard_map/ppermute | solution.py:30
  484.3 32.4 %collective-permute-start.11 = (bf16[4,128,768]{2,1,0:T(8,128)(2,1)S(1)}, bf16[4,128,768]{2,1,0:T(8,128)(2,1)S(1)}, u32[]{:S(2)}, u32[]{:S(2)}) collective-permute-start(bf16[4,128,768]{2,1,0:T(8,128)(2,1)S(1)} %collective-permute-done.9), channel_id=1, source_target_pairs={{0,1},{1,2},{2,3},{3,0},{4,5},{5,6},{6,7},{7,4},{8,9},{9,10},{10,1... | collective-permute-start | bytes 2359304 | tf_op jit(solution)/shard_map/ppermute | solution.py:27
  542.6 214.3 %reduce-scatter.17.cloned.1.call-start = ((), (), s32[]{:S(2)}) async-start(), calls=%async_computation.12 | async-start | bytes 7864320 | tf_op jit(solution)/shard_map/reduce_scatter | solution.py:55
  616.2 54.7 %slice-start.4 = ((s8[6291456]{0:T(1024)(128)(4,1)}), s8[4194304]{0:T(1024)(128)(4,1)S(1)}, s32[]{:S(2)}) async-start(s8[6291456]{0:T(1024)(128)(4,1)} %bitcast.493), calls=%async_computation.21 | async-start | bytes 8388608
  616.5 54.5 %slice-start.5 = ((s8[6291456]{0:T(1024)(128)(4,1)}), s8[2097152]{0:T(1024)(128)(4,1)S(1)}, s32[]{:S(2)}) async-start(s8[6291456]{0:T(1024)(128)(4,1)} %bitcast.493), calls=%async_computation.22 | async-start | bytes 4194304
  617.1 53.9 %copy-start.90 = (bf16[2,768,768]{2,1,0:T(8,128)(2,1)S(1)}, bf16[2,768,768]{2,1,0:T(8,128)(2,1)}, u32[]{:S(2)}) copy-start(bf16[2,768,768]{2,1,0:T(8,128)(2,1)} %param.38) | copy-start | bytes 7077892
  617.1 21.4 %collective-permute-start.12 = (bf16[4,128,768]{2,1,0:T(8,128)(2,1)S(1)}, bf16[4,128,768]{2,1,0:T(8,128)(2,1)S(1)}, u32[]{:S(2)}, u32[]{:S(2)}) collective-permute-start(bf16[4,128,768]{2,1,0:T(8,128)(2,1)S(1)} %get-tuple-element.349), channel_id=1, source_target_pairs={{0,1},{1,2},{2,3},{3,0},{4,5},{5,6},{6,7},{7,4},{8,9},{9,10},{10,1... | collective-permute-start | bytes 2359304 | tf_op jit(solution)/shard_map/ppermute | solution.py:27
  618.6 36.7 %collective-permute-start.13 = (bf16[4,128,768]{2,1,0:T(8,128)(2,1)S(1)}, bf16[4,128,768]{2,1,0:T(8,128)(2,1)S(1)}, u32[]{:S(2)}, u32[]{:S(2)}) collective-permute-start(bf16[4,128,768]{2,1,0:T(8,128)(2,1)S(1)} %get-tuple-element.349), channel_id=1, source_target_pairs={{0,3},{1,0},{2,1},{3,2},{4,7},{5,4},{6,5},{7,6},{8,11},{9,8},{10,9... | collective-permute-start | bytes 2359304 | tf_op jit(solution)/shard_map/ppermute | solution.py:30
  638.5 32.4 %collective-permute-start.14 = (bf16[4,128,768]{2,1,0:T(8,128)(2,1)S(1)}, bf16[4,128,768]{2,1,0:T(8,128)(2,1)S(1)}, u32[]{:S(2)}, u32[]{:S(2)}) collective-permute-start(bf16[4,128,768]{2,1,0:T(8,128)(2,1)S(1)} %collective-permute-done.12), channel_id=1, source_target_pairs={{0,1},{1,2},{2,3},{3,0},{4,5},{5,6},{6,7},{7,4},{8,9},{9,10},{10,1... | collective-permute-start | bytes 2359304 | tf_op jit(solution)/shard_map/ppermute | solution.py:27
  686.7 268.3 %reduce-scatter.19.cloned.1.call-start = ((), (), s32[]{:S(2)}) async-start(), calls=%async_computation.13 | async-start | bytes 7864320 | tf_op jit(solution)/shard_map/reduce_scatter | solution.py:55
  765.5 21.5 %collective-permute-start.15 = (bf16[4,128,768]{2,1,0:T(8,128)(2,1)}, bf16[4,128,768]{2,1,0:T(8,128)(2,1)S(1)}, u32[]{:S(2)}, u32[]{:S(2)}) collective-permute-start(bf16[4,128,768]{2,1,0:T(8,128)(2,1)} %get-tuple-element.344), channel_id=1, source_target_pairs={{0,1},{1,2},{2,3},{3,0},{4,5},{5,6},{6,7},{7,4},{8,9},{9,10},{10,1... | collective-permute-start | bytes 2359304 | tf_op jit(solution)/shard_map/ppermute | solution.py:27
  767.0 36.9 %collective-permute-start.16 = (bf16[4,128,768]{2,1,0:T(8,128)(2,1)}, bf16[4,128,768]{2,1,0:T(8,128)(2,1)S(1)}, u32[]{:S(2)}, u32[]{:S(2)}) collective-permute-start(bf16[4,128,768]{2,1,0:T(8,128)(2,1)} %get-tuple-element.344), channel_id=1, source_target_pairs={{0,3},{1,0},{2,1},{3,2},{4,7},{5,4},{6,5},{7,6},{8,11},{9,8},{10,9... | collective-permute-start | bytes 2359304 | tf_op jit(solution)/shard_map/ppermute | solution.py:30
  787.0 32.5 %collective-permute-start.17 = (bf16[4,128,768]{2,1,0:T(8,128)(2,1)S(1)}, bf16[4,128,768]{2,1,0:T(8,128)(2,1)}, u32[]{:S(2)}, u32[]{:S(2)}) collective-permute-start(bf16[4,128,768]{2,1,0:T(8,128)(2,1)S(1)} %collective-permute-done.15), channel_id=1, source_target_pairs={{0,1},{1,2},{2,3},{3,0},{4,5},{5,6},{6,7},{7,4},{8,9},{9,10},{10,1... | collective-permute-start | bytes 2359304 | tf_op jit(solution)/shard_map/ppermute | solution.py:27
  787.6 34.0 %copy-start.59 = (bf16[2,192,768]{2,1,0:T(8,128)(2,1)S(1)}, bf16[2,192,768]{2,1,0:T(8,128)(2,1)}, u32[]{:S(2)}) copy-start(bf16[2,192,768]{2,1,0:T(8,128)(2,1)} %param.32) | copy-start | bytes 1769476
  872.2 72.7 %copy-start.86 = (s32[64]{0:T(128)S(1)}, s32[64]{0:T(128)}, u32[]{:S(2)}) copy-start(s32[64]{0:T(128)} %param.29) | copy-start | bytes 772
  872.2 223.8 %reduce-scatter.21.cloned.1.call-start = ((), (), s32[]{:S(2)}) async-start(), calls=%async_computation.14 | async-start | bytes 7864320 | tf_op jit(solution)/shard_map/reduce_scatter | solution.py:55
  872.9 82.2 %copy-start.10 = (f32[4,128,768]{2,1,0:T(8,128)S(1)}, f32[4,128,768]{2,1,0:T(8,128)}, u32[]{:S(2)}) copy-start(f32[4,128,768]{2,1,0:T(8,128)} %copy-done.9) | copy-start | bytes 4718596
  955.0 58.5 %slice-start.2 = ((s8[6291456]{0:T(1024)(128)(4,1)}), s8[4194304]{0:T(1024)(128)(4,1)S(1)}, s32[]{:S(2)}) async-start(s8[6291456]{0:T(1024)(128)(4,1)} %bitcast.491), calls=%async_computation.19 | async-start | bytes 8388608
  958.7 54.9 %slice-start = ((s8[6291456]{0:T(1024)(128)(4,1)}), s8[4194304]{0:T(1024)(128)(4,1)S(1)}, s32[]{:S(2)}) async-start(s8[6291456]{0:T(1024)(128)(4,1)} %bitcast.489), calls=%async_computation.17 | async-start | bytes 8388608
  958.7 54.9 %slice-start.3 = ((s8[6291456]{0:T(1024)(128)(4,1)}), s8[2097152]{0:T(1024)(128)(4,1)S(1)}, s32[]{:S(2)}) async-start(s8[6291456]{0:T(1024)(128)(4,1)} %bitcast.491), calls=%async_computation.20 | async-start | bytes 4194304
  959.3 54.3 %slice-start.1 = ((s8[6291456]{0:T(1024)(128)(4,1)}), s8[2097152]{0:T(1024)(128)(4,1)S(1)}, s32[]{:S(2)}) async-start(s8[6291456]{0:T(1024)(128)(4,1)} %bitcast.489), calls=%async_computation.18 | async-start | bytes 4194304
  959.7 53.9 %copy-start.77 = (f32[768]{0:T(1024)S(1)}, f32[768]{0:T(1024)}, u32[]{:S(2)}) copy-start(f32[768]{0:T(1024)} %copy-done.76) | copy-start | bytes 9220
  959.7 53.9 %copy-start.91 = (bf16[2,768,768]{2,1,0:T(8,128)(2,1)S(1)}, bf16[2,768,768]{2,1,0:T(8,128)(2,1)}, u32[]{:S(2)}) copy-start(bf16[2,768,768]{2,1,0:T(8,128)(2,1)} %param.38) | copy-start | bytes 7077892
  959.7 21.4 %collective-permute-start.18 = (bf16[4,128,768]{2,1,0:T(8,128)(2,1)S(1)}, bf16[4,128,768]{2,1,0:T(8,128)(2,1)S(1)}, u32[]{:S(2)}, u32[]{:S(2)}) collective-permute-start(bf16[4,128,768]{2,1,0:T(8,128)(2,1)S(1)} %get-tuple-element.340), channel_id=1, source_target_pairs={{0,1},{1,2},{2,3},{3,0},{4,5},{5,6},{6,7},{7,4},{8,9},{9,10},{10,1... | collective-permute-start | bytes 2359304 | tf_op jit(solution)/shard_map/ppermute | solution.py:27
  960.6 37.3 %collective-permute-start.19 = (bf16[4,128,768]{2,1,0:T(8,128)(2,1)S(1)}, bf16[4,128,768]{2,1,0:T(8,128)(2,1)S(1)}, u32[]{:S(2)}, u32[]{:S(2)}) collective-permute-start(bf16[4,128,768]{2,1,0:T(8,128)(2,1)S(1)} %get-tuple-element.340), channel_id=1, source_target_pairs={{0,3},{1,0},{2,1},{3,2},{4,7},{5,4},{6,5},{7,6},{8,11},{9,8},{10,9... | collective-permute-start | bytes 2359304 | tf_op jit(solution)/shard_map/ppermute | solution.py:30
  981.1 32.4 %collective-permute-start.20 = (bf16[4,128,768]{2,1,0:T(8,128)(2,1)S(1)}, bf16[4,128,768]{2,1,0:T(8,128)(2,1)S(1)}, u32[]{:S(2)}, u32[]{:S(2)}) collective-permute-start(bf16[4,128,768]{2,1,0:T(8,128)(2,1)S(1)} %collective-permute-done.18), channel_id=1, source_target_pairs={{0,1},{1,2},{2,3},{3,0},{4,5},{5,6},{6,7},{7,4},{8,9},{9,10},{10,1... | collective-permute-start | bytes 2359304 | tf_op jit(solution)/shard_map/ppermute | solution.py:27
  1025.7 467.8 %all-reduce.5.cloned.1.call-start = ((), (), s32[]{:S(2)}) async-start(), calls=%async_computation.16 | async-start | bytes 28311552 | tf_op jit(solution)/shard_map/psum | solution.py:380
  1044.5 51.6 %copy-start.7 = (f32[4,128,768]{2,1,0:T(8,128)S(1)}, f32[4,128,768]{2,1,0:T(8,128)}, u32[]{:S(2)}) copy-start(f32[4,128,768]{2,1,0:T(8,128)} %copy-done.6) | copy-start | bytes 4718596
  1044.5 51.6 %copy-start.63 = (f32[768]{0:T(1024)S(1)}, f32[768]{0:T(1024)}, u32[]{:S(2)}) copy-start(f32[768]{0:T(1024)} %copy-done.62) | copy-start | bytes 9220
  1044.5 51.6 %copy-start.65 = (f32[4,128]{1,0:T(4,128)S(1)}, f32[4,128]{1,0:T(4,128)}, u32[]{:S(2)}) copy-start(f32[4,128]{1,0:T(4,128)} %copy-done.64) | copy-start | bytes 6148
  1044.5 51.5 %copy-start.69 = (f32[4,128]{1,0:T(4,128)S(1)}, f32[4,128]{1,0:T(4,128)}, u32[]{:S(2)}) copy-start(f32[4,128]{1,0:T(4,128)} %copy-done.68) | copy-start | bytes 6148
  1046.1 52.2 %copy-start.73 = (f32[4,128]{1,0:T(4,128)S(1)}, f32[4,128]{1,0:T(4,128)}, u32[]{:S(2)}) copy-start(f32[4,128]{1,0:T(4,128)} %copy-done.72) | copy-start | bytes 6148
  1100.2 21.3 %collective-permute-start.21 = (bf16[4,128,768]{2,1,0:T(8,128)(2,1)S(1)}, bf16[4,128,768]{2,1,0:T(8,128)(2,1)S(1)}, u32[]{:S(2)}, u32[]{:S(2)}) collective-permute-start(bf16[4,128,768]{2,1,0:T(8,128)(2,1)S(1)} %get-tuple-element.335), channel_id=1, source_target_pairs={{0,1},{1,2},{2,3},{3,0},{4,5},{5,6},{6,7},{7,4},{8,9},{9,10},{10,1... | collective-permute-start | bytes 2359304 | tf_op jit(solution)/shard_map/ppermute | solution.py:27
  1107.5 30.8 %collective-permute-start.22 = (bf16[4,128,768]{2,1,0:T(8,128)(2,1)S(1)}, bf16[4,128,768]{2,1,0:T(8,128)(2,1)S(1)}, u32[]{:S(2)}, u32[]{:S(2)}) collective-permute-start(bf16[4,128,768]{2,1,0:T(8,128)(2,1)S(1)} %get-tuple-element.335), channel_id=1, source_target_pairs={{0,3},{1,0},{2,1},{3,2},{4,7},{5,4},{6,5},{7,6},{8,11},{9,8},{10,9... | collective-permute-start | bytes 2359304 | tf_op jit(solution)/shard_map/ppermute | solution.py:30
  1121.5 32.4 %collective-permute-start.23 = (bf16[4,128,768]{2,1,0:T(8,128)(2,1)S(1)}, bf16[4,128,768]{2,1,0:T(8,128)(2,1)S(1)}, u32[]{:S(2)}, u32[]{:S(2)}) collective-permute-start(bf16[4,128,768]{2,1,0:T(8,128)(2,1)S(1)} %collective-permute-done.21), channel_id=1, source_target_pairs={{0,1},{1,2},{2,3},{3,0},{4,5},{5,6},{6,7},{7,4},{8,9},{9,10},{10,1... | collective-permute-start | bytes 2359304 | tf_op jit(solution)/shard_map/ppermute | solution.py:27
  1160.5 41.8 %copy-start.3 = (bf16[4,512,768]{2,1,0:T(8,128)(2,1)S(1)}, bf16[4,512,768]{2,1,0:T(8,128)(2,1)}, u32[]{:S(2)}) copy-start(bf16[4,512,768]{2,1,0:T(8,128)(2,1)} %copy-done.2) | copy-start | bytes 9437188
  1208.3 358.4 %reduce-scatter.23.cloned.1.call-start = ((), (), s32[]{:S(2)}) async-start(), calls=%async_computation.15 | async-start | bytes 7864320 | tf_op jit(solution)/shard_map/reduce_scatter | solution.py:55
  1504.2 62.5 %copy-start.19 = (f32[4,128,768]{2,1,0:T(8,128)S(1)}, f32[4,128,768]{2,1,0:T(8,128)}, u32[]{:S(2)}) copy-start(f32[4,128,768]{2,1,0:T(8,128)} %copy-done.18) | copy-start | bytes 4718596
  (75 other events, 434.9 us)
Sparse Core Ops, SparseCore 0:
  82.1 70.5 reduce-scatter.8
  235.3 70.0 reduce-scatter.10
  388.9 70.0 reduce-scatter.12
  542.7 70.0 reduce-scatter.14
  686.8 70.0 reduce-scatter.16
  872.3 82.6 reduce-scatter.18
  1025.8 70.1 reduce-scatter.20
  1208.4 284.9 all-reduce.4
  1496.5 70.1 reduce-scatter.22
